TPU v7x, 32 devices: a whole 2x2x4 slice. The times are simulated.
32 devices in a mesh: expert: 8 (over z, core), tensor: 4 (over y, x).
Axes of the slice: x: 2, y: 2, z: 4, core: 2. Of those that a mesh axis runs over, the one named last changes fastest.
Arguments:
- tokens: bfloat16 [256, 4096], P('expert', 'tensor'), may hold values from -6 to 6
- cotangent: bfloat16 [256, 4096], P('expert', 'tensor'), may hold values from -6 to 6
- expert_ids: int32 [256, 8], P('expert'), may hold values from 0 to 63, all different within a row; in each aligned block of 32 rows (0 to 31, 32 to 63, ...) at most 8 rows name the same one
- route_weight: float32 [256, 8], P('expert'), may hold values from 0.05 to 0.25
- w_gate: bfloat16 [64, 4096, 1536], P('expert', 'tensor'), may hold values from -0.09375 to 0.09375
- w_up: bfloat16 [64, 4096, 1536], P('expert', 'tensor'), may hold values from -0.09375 to 0.09375
- w_down: bfloat16 [64, 1536, 4096], P('expert', None, 'tensor'), may hold values from -0.15625 to 0.15625
Outputs:
- mixed_out: bfloat16 [256, 4096], P('expert', 'tensor')
- input_grad: bfloat16 [256, 4096], P('expert', 'tensor')
- down_grad: bfloat16 [64, 1536, 4096], P('expert', None, 'tensor')
Inputs may be any that keep to these rules, and one draw needn't show every extreme that they name: `expert_ids`: each row names 8 different experts; within the 32 rows of one device no expert is named more than 8 times.
All inputs are finite; a program needn't handle non-finite values.
Results may differ from a plain program's by a relative error of at most 0.023.
Values may be sent and summed in bfloat16 or wider, within the bound.
No kernel may reach another device: no remote copies, remote signals or barrier semaphores. Data moves between devices by JAX's collectives and lax.ppermute only.
A program may use at most 192 MiB of HBM per device.

v0:
```python
import jax
import jax.numpy as jnp
from jax import lax
from jax.sharding import PartitionSpec as P


def local(tokens, cotangent, expert_ids, route_weight, w_gate, w_up, w_down):
    resident_specialists = w_gate.shape[0]
    experts = resident_specialists * lax.axis_size("expert")
    tok_count = expert_ids.shape[0]
    top_count = expert_ids.shape[1]
    capacity = 2 * tok_count * top_count // experts
    model_width = tokens.shape[1]
    flat_ids = expert_ids.reshape(-1)
    onehot = (flat_ids[:, None] == jnp.arange(experts, dtype=jnp.int32)[None, :]).astype(jnp.int32)
    before = jnp.cumsum(onehot, axis=0) - onehot
    slot_index = jnp.sum(before * onehot, axis=1)
    target = flat_ids * capacity + slot_index
    chosen = (target[:, None] == jnp.arange(experts * capacity, dtype=jnp.int32)[None, :]).astype(
        jnp.float32
    )
    chosen = chosen.reshape(tok_count, top_count, experts * capacity)
    expert_assignment = jnp.sum(chosen, axis=1)
    weighted = jnp.sum(chosen * route_weight[:, :, None], axis=1)
    token_send = jnp.dot(
        expert_assignment.T.astype(jnp.bfloat16), tokens, preferred_element_type=jnp.float32
    )
    token_send = token_send.astype(jnp.bfloat16).reshape(experts, capacity, model_width)
    gradient_outgoing = jnp.dot(
        weighted.T, cotangent, precision=lax.Precision.HIGHEST, preferred_element_type=jnp.float32
    )
    gradient_outgoing = gradient_outgoing.astype(jnp.bfloat16).reshape(
        experts, capacity, model_width
    )
    token_rows, grad_rows = (
        lax.all_to_all(token_send, "expert", split_axis=0, concat_axis=1, tiled=True),
        lax.all_to_all(gradient_outgoing, "expert", split_axis=0, concat_axis=1, tiled=True),
    )
    pre_gate = jnp.einsum("erd,edf->erf", token_rows, w_gate, preferred_element_type=jnp.float32)
    pre_up = jnp.einsum("erd,edf->erf", token_rows, w_up, preferred_element_type=jnp.float32)
    slice_breadth = w_gate.shape[2] // lax.axis_size("tensor")
    gate_sum, up_sum = (
        lax.psum(pre_gate.astype(jnp.bfloat16), "tensor").astype(jnp.float32),
        lax.psum(pre_up.astype(jnp.bfloat16), "tensor").astype(jnp.float32),
    )
    sigmoid_all = jax.nn.sigmoid(gate_sum)
    hidden = (gate_sum * sigmoid_all * up_sum).astype(jnp.bfloat16)
    out_rows = jnp.einsum(
        "erf,efd->erd", hidden, w_down, preferred_element_type=jnp.float32
    ).astype(jnp.bfloat16)
    down_grad = jnp.einsum("erf,erd->efd", hidden, grad_rows, preferred_element_type=jnp.float32)
    offset = lax.axis_index("tensor") * slice_breadth
    gate_part = lax.dynamic_slice_in_dim(gate_sum, offset, slice_breadth, 2)
    up_part = lax.dynamic_slice_in_dim(up_sum, offset, slice_breadth, 2)
    sigmoid_part = lax.dynamic_slice_in_dim(sigmoid_all, offset, slice_breadth, 2)
    hidden_term = jnp.einsum("erd,efd->erf", grad_rows, w_down, preferred_element_type=jnp.float32)
    hidden_grad = lax.psum_scatter(
        hidden_term.astype(jnp.bfloat16), "tensor", scatter_dimension=2, tiled=True
    ).astype(jnp.float32)
    gate_grad = (
        hidden_grad * up_part * sigmoid_part * (1.0 + gate_part * (1.0 - sigmoid_part))
    ).astype(jnp.bfloat16)
    up_grad = (hidden_grad * gate_part * sigmoid_part).astype(jnp.bfloat16)
    gate_piece = lax.all_gather(gate_grad, "tensor", axis=2, tiled=True)
    up_piece = lax.all_gather(up_grad, "tensor", axis=2, tiled=True)
    running = jnp.einsum("erf,edf->erd", gate_piece, w_gate, preferred_element_type=jnp.float32)
    input_rows = running + jnp.einsum(
        "erf,edf->erd", up_piece, w_up, preferred_element_type=jnp.float32
    )
    input_rows = input_rows.astype(jnp.bfloat16)
    returned_out, returned_in = (
        lax.all_to_all(out_rows, "expert", split_axis=1, concat_axis=0, tiled=True),
        lax.all_to_all(input_rows, "expert", split_axis=1, concat_axis=0, tiled=True),
    )
    returned_out = returned_out.reshape(experts * capacity, model_width)
    returned_in = returned_in.reshape(experts * capacity, model_width)
    mixed_out = jnp.dot(
        weighted, returned_out, precision=lax.Precision.HIGHEST, preferred_element_type=jnp.float32
    )
    input_grad = jnp.dot(
        expert_assignment.astype(jnp.bfloat16), returned_in, preferred_element_type=jnp.float32
    )
    return (
        mixed_out.astype(jnp.bfloat16),
        input_grad.astype(jnp.bfloat16),
        down_grad.astype(jnp.bfloat16),
    )


def solution(mesh):
    return jax.shard_map(
        local,
        mesh=mesh,
        in_specs=(
            P("expert", "tensor"),
            P("expert", "tensor"),
            P("expert", None),
            P("expert", None),
            P("expert", "tensor", None),
            P("expert", "tensor", None),
            P("expert", None, "tensor"),
        ),
        out_specs=(P("expert", "tensor"), P("expert", "tensor"), P("expert", None, "tensor")),
        check_vma=False,
    )
```

profile of v0, /device:TPU:0, one launch (start us, length us, event | category | flops | bytes accessed | tf_op | source)
XLA Modules:
  0.0 326.9 jit_solution(5938493697258200641)
XLA Ops:
  7.2 0.8 copy.45
  8.0 0.1 eq.43
  8.1 0.1 eq.39
  8.2 0.8 copy.49
  8.9 0.6 reduce-window.6
  9.6 0.2 slice_reduce_fusion
  9.8 0.1 fusion.17
  9.9 0.1 reduce_sum.30
  10.0 0.4 convert_reduce_fusion
  10.4 0.6 copy-done.4
  11.0 1.4 fusion
  12.4 6.4 %all-to-all-start = ((bf16[64,8,1024]{2,1,0:T(8,128)(2,1)}), bf16[64,8,1024]{2,1,0:T(8,128)(2,1)S(1)}, u32[]{:S(2)}, u32[]{:S(2)}) async-start(bf16[64,8,1024]{2,1,0:T(8,128)(2,1)} %fusion), calls=%async_computation | async-start | bytes 2097152 | tf_op jit(solution)/shard_map/all_to_all | solution.py:36
  18.8 2.0 fusion.1
  20.8 24.5 %all-to-all-done = bf16[64,8,1024]{2,1,0:T(8,128)(2,1)S(1)} async-done(((bf16[64,8,1024]{2,1,0:T(8,128)(2,1)}), bf16[64,8,1024]{2,1,0:T(8,128)(2,1)S(1)}, u32[]{:S(2)}, u32[]{:S(2)}) %all-to-all-start) | async-done | bytes 1048608 | tf_op jit(solution)/shard_map/all_to_all | solution.py:36
  45.4 3.6 %all-to-all-start.2 = ((bf16[64,8,1024]{2,1,0:T(8,128)(2,1)}), bf16[64,8,1024]{2,1,0:T(8,128)(2,1)S(1)}, u32[]{:S(2)}, u32[]{:S(2)}) async-start(bf16[64,8,1024]{2,1,0:T(8,128)(2,1)} %fusion.1), calls=%async_computation.2 | async-start | bytes 2097152 | tf_op jit(solution)/shard_map/all_to_all | solution.py:37
  48.9 0.0 all-reduce.3.cloned.1.call-start
  49.0 13.7 %convolution_convert_fusion.2 = bf16[8,64,1536]{2,1,0:T(8,128)(2,1)} fusion(bf16[8,1024,1536]{2,1,0:T(8,128)(2,1)} %param.12, bf16[8,8,8,1024]{3,2,1,0:T(8,128)(2,1)S(1)} %bitcast.68), kind=kOutput, calls=%fused_computation.4 | convolution fusion | flops 1611399168 | bytes 27787264 | tf_op jit(solution)/shard_map/erd,edf->erf/dot_general | solution.py:40
  62.7 13.7 %convolution_convert_fusion.3 = bf16[8,64,1536]{2,1,0:T(8,128)(2,1)} fusion(bf16[8,1024,1536]{2,1,0:T(8,128)(2,1)} %param.11, bf16[8,8,8,1024]{3,2,1,0:T(8,128)(2,1)S(1)} %bitcast.69), kind=kOutput, calls=%fused_computation.5 | convolution fusion | flops 1611399168 | bytes 27787264 | tf_op jit(solution)/shard_map/erd,edf->erf/dot_general | solution.py:39
  76.4 0.0 reduce-scatter.4.cloned.1.call-start
  76.5 13.2 %convolution_convert_fusion.1 = bf16[8,64,1536]{2,1,0:T(8,128)(2,1)S(1)} fusion(bf16[8,1536,1024]{2,1,0:T(8,128)(2,1)} %param.13, bf16[8,8,8,1024]{3,2,1,0:T(8,128)(2,1)S(1)} %bitcast.65), kind=kOutput, calls=%fused_computation.3 | convolution fusion | flops 1611399168 | bytes 27787264 | tf_op jit(solution)/shard_map/erd,efd->erf/dot_general | solution.py:56
  89.7 3.5 %copy.60 = bf16[8,64,1536]{1,0,2:T(8,128)(2,1)} copy(bf16[8,64,1536]{2,1,0:T(8,128)(2,1)S(1)} %convolution_convert_fusion.1) | data formatting | bytes 3145728
  93.2 5.4 %reshape.61 = bf16[1536,512]{1,0:T(8,128)(2,1)} reshape(bf16[1536,8,64]{2,1,0:T(8,128)(2,1)} %bitcast.67) | data formatting | bytes 3145728
  98.6 0.2 all-gather.3.cloned.1.call-start
  98.9 66.0 %all-reduce.3.cloned.1.call-done = (bf16[8,64,1536]{2,1,0:T(8,128)(2,1)}, bf16[8,64,1536]{2,1,0:T(8,128)(2,1)}) async-done(((bf16[8,64,1536]{2,1,0:T(8,128)(2,1)}, bf16[8,64,1536]{2,1,0:T(8,128)(2,1)}), (bf16[8,64,1536]{2,1,0:T(8,128)(2,1)}, bf16[8,64,1536]{2,1,0:T(8,128)(2,1)})) %all-reduce.3.cloned.1.call-update) | async-done | bytes 3145744 | tf_op jit(solution)/shard_map/psum | solution.py:43
  164.9 3.6 %convert_element_type.70 = f32[8,64,1536]{2,1,0:T(8,128)} convert(bf16[8,64,1536]{2,1,0:T(8,128)(2,1)} %get-tuple-element.5) | non-fusion elementwise | flops 786432 | bytes 4718592 | tf_op jit(solution)/shard_map/convert_element_type | solution.py:43
  168.5 2.5 add_divide_fusion
  171.0 28.1 %reduce-scatter.4.cloned.1.call-done = bf16[384,512]{1,0:T(8,128)(2,1)} async-done(((bf16[1536,512]{1,0:T(8,128)(2,1)}), bf16[384,512]{1,0:T(8,128)(2,1)}) %reduce-scatter.4.cloned.1.call-update) | async-done | bytes 393232
  199.0 1.5 reshape.62
  200.6 1.3 copy.61
  201.8 1.8 convert_element_type.72
  203.7 2.6 fusion.14
  206.3 0.0 all-gather.5.cloned.1.call-start
  206.4 0.5 all-gather.5.cloned.1.call-update
  206.9 13.5 %convolution_convert_fusion.4 = bf16[8,64,1024]{2,1,0:T(8,128)(2,1)S(1)} fusion(bf16[8,1536,1024]{2,1,0:T(8,128)(2,1)} %param.13, bf16[8,64,1536]{2,1,0:T(8,128)(2,1)S(1)} %copy-done.2, bf16[8,64,1536]{2,1,0:T(8,128)(2,1)} %get-tuple-element.6), kind=kOutput, calls=%fused_computation.7 | convolution fusion | flops 1617428480 | bytes 29360128 | tf_op jit(solution)/shard_map/erf,efd->erd/dot_general | solution.py:48
  220.4 1.6 copy.51
  222.0 4.6 %all-to-all-start.1 = ((bf16[8,64,1024]{2,0,1:T(8,128)(2,1)}), bf16[8,64,1024]{2,0,1:T(8,128)(2,1)}, u32[]{:S(2)}, u32[]{:S(2)}) async-start(bf16[8,64,1024]{2,0,1:T(8,128)(2,1)} %copy.51), calls=%async_computation.1 | async-start | bytes 2097152 | tf_op jit(solution)/shard_map/all_to_all | solution.py:72
  226.6 10.6 %all-gather.3.cloned.1.call-done = bf16[8,64,1536]{2,1,0:T(8,128)(2,1)} async-done(((bf16[8,64,384]{2,1,0:T(8,128)(2,1)}), bf16[8,64,1536]{2,1,0:T(8,128)(2,1)}) %all-gather.3.cloned.1.call-update) | async-done | bytes 1572880 | tf_op jit(solution)/shard_map/all_gather | solution.py:64
  237.2 13.8 %fusion.21 = f32[8,64,1024]{2,1,0:T(8,128)} fusion(bf16[8,64,1536]{2,1,0:T(8,128)(2,1)} %all-gather.3.cloned.1.call-done, bf16[8,1024,1536]{2,1,0:T(8,128)(2,1)} %param.11), kind=kOutput, calls=%fused_computation.44 | convolution fusion | flops 1610612736 | bytes 28835840 | tf_op jit(solution)/shard_map/erf,edf->erd/dot_general | solution.py:66
  251.0 18.6 %all-gather.5.cloned.1.call-done = bf16[8,64,1536]{2,1,0:T(8,128)(2,1)} async-done(((bf16[8,64,384]{2,1,0:T(8,128)(2,1)}), bf16[8,64,1536]{2,1,0:T(8,128)(2,1)}) %all-gather.5.cloned.1.call-update) | async-done | bytes 1572880 | tf_op jit(solution)/shard_map/all_gather | solution.py:65
  269.6 14.0 %add_convert_fusion = bf16[8,64,1024]{2,1,0:T(8,128)(2,1)} fusion(f32[8,64,1024]{2,1,0:T(8,128)} %fusion.21, bf16[8,64,1536]{2,1,0:T(8,128)(2,1)} %all-gather.5.cloned.1.call-done, bf16[8,1024,1536]{2,1,0:T(8,128)(2,1)} %param.12), kind=kOutput, calls=%fused_computation.6 | convolution fusion | flops 1611661312 | bytes 29884416 | tf_op jit(solution)/shard_map/erf,edf->erd/dot_general | solution.py:67
  283.6 2.8 copy.55
  286.3 4.6 %all-to-all-start.3 = ((bf16[8,64,1024]{2,0,1:T(8,128)(2,1)}), bf16[8,64,1024]{2,0,1:T(8,128)(2,1)}, u32[]{:S(2)}, u32[]{:S(2)}) async-start(bf16[8,64,1024]{2,0,1:T(8,128)(2,1)} %copy.55), calls=%async_computation.3 | async-start | bytes 2097152 | tf_op jit(solution)/shard_map/all_to_all | solution.py:73
  291.0 13.8 %convolution_convert_fusion = bf16[8,1536,1024]{2,1,0:T(8,128)(2,1)} fusion(bf16[8,8,8,1024]{3,2,1,0:T(8,128)(2,1)S(1)} %bitcast.66, bf16[8,64,1536]{2,1,0:T(8,128)(2,1)S(1)} %copy-done.2, bf16[8,64,1536]{2,1,0:T(8,128)(2,1)} %get-tuple-element.6), kind=kOutput, calls=%fused_computation | convolution fusion | flops 1629487104 | bytes 29360128 | tf_op jit(solution)/shard_map/erf,erd->efd/dot_general | solution.py:51
  304.8 1.9 copy.53
  306.6 1.2 convolution_convert_fusion.8
  307.9 9.8 %all-to-all-done.3 = bf16[8,64,1024]{2,0,1:T(8,128)(2,1)} async-done(((bf16[8,64,1024]{2,0,1:T(8,128)(2,1)}), bf16[8,64,1024]{2,0,1:T(8,128)(2,1)}, u32[]{:S(2)}, u32[]{:S(2)}) %all-to-all-start.3) | async-done | bytes 1048608 | tf_op jit(solution)/shard_map/all_to_all | solution.py:73
  317.6 1.8 copy.57
  319.5 0.9 convolution_convert_fusion.7
  (22 shorter events, 0.2 us)
Async XLA Ops:
  7.2 3.9 %copy-start = (bf16[32,1024]{1,0:T(8,128)(2,1)S(1)}, bf16[32,1024]{1,0:T(8,128)(2,1)}, u32[]{:S(2)}) copy-start(bf16[32,1024]{1,0:T(8,128)(2,1)} %param.7) | copy-start | bytes 196612
  7.2 11.6 %copy-start.6 = (bf16[32,1024]{1,0:T(8,128)(2,1)S(1)}, bf16[32,1024]{1,0:T(8,128)(2,1)}, u32[]{:S(2)}) copy-start(bf16[32,1024]{1,0:T(8,128)(2,1)} %param.8) | copy-start | bytes 196612
  10.4 0.6 copy-start.4
  12.4 32.9 %all-to-all-start = ((bf16[64,8,1024]{2,1,0:T(8,128)(2,1)}), bf16[64,8,1024]{2,1,0:T(8,128)(2,1)S(1)}, u32[]{:S(2)}, u32[]{:S(2)}) async-start(bf16[64,8,1024]{2,1,0:T(8,128)(2,1)} %fusion), calls=%async_computation | async-start | bytes 2097152 | tf_op jit(solution)/shard_map/all_to_all | solution.py:36
  45.4 31.1 %all-to-all-start.2 = ((bf16[64,8,1024]{2,1,0:T(8,128)(2,1)}), bf16[64,8,1024]{2,1,0:T(8,128)(2,1)S(1)}, u32[]{:S(2)}, u32[]{:S(2)}) async-start(bf16[64,8,1024]{2,1,0:T(8,128)(2,1)} %fusion.1), calls=%async_computation.2 | async-start | bytes 2097152 | tf_op jit(solution)/shard_map/all_to_all | solution.py:37
  48.9 116.0 %all-reduce.3.cloned.1.call-start = ((), (), s32[]{:S(2)}) async-start(), calls=%async_computation.8 | async-start | bytes 6291456 | tf_op jit(solution)/shard_map/psum | solution.py:43
  76.4 122.6 %reduce-scatter.4.cloned.1.call-start = ((), (), s32[]{:S(2)}) async-start(), calls=%async_computation.7 | async-start | bytes 1966080
  98.6 138.5 %all-gather.3.cloned.1.call-start = ((), (), s32[]{:S(2)}) async-start(), calls=%async_computation.5 | async-start | bytes 1966080 | tf_op jit(solution)/shard_map/all_gather | solution.py:64
  164.9 3.6 %copy-start.2 = (bf16[8,64,1536]{2,1,0:T(8,128)(2,1)S(1)}, bf16[8,64,1536]{2,1,0:T(8,128)(2,1)}, u32[]{:S(2)}) copy-start(bf16[8,64,1536]{2,1,0:T(8,128)(2,1)} %get-tuple-element.5) | copy-start | bytes 4718596
  201.8 1.9 copy-start.3
  206.3 63.3 %all-gather.5.cloned.1.call-start = ((), (), s32[]{:S(2)}) async-start(), calls=%async_computation.6 | async-start | bytes 1966080 | tf_op jit(solution)/shard_map/all_gather | solution.py:65
  222.0 64.3 %all-to-all-start.1 = ((bf16[8,64,1024]{2,0,1:T(8,128)(2,1)}), bf16[8,64,1024]{2,0,1:T(8,128)(2,1)}, u32[]{:S(2)}, u32[]{:S(2)}) async-start(bf16[8,64,1024]{2,0,1:T(8,128)(2,1)} %copy.51), calls=%async_computation.1 | async-start | bytes 2097152 | tf_op jit(solution)/shard_map/all_to_all | solution.py:72
  286.3 31.3 %all-to-all-start.3 = ((bf16[8,64,1024]{2,0,1:T(8,128)(2,1)}), bf16[8,64,1024]{2,0,1:T(8,128)(2,1)}, u32[]{:S(2)}, u32[]{:S(2)}) async-start(bf16[8,64,1024]{2,0,1:T(8,128)(2,1)} %copy.55), calls=%async_computation.3 | async-start | bytes 2097152 | tf_op jit(solution)/shard_map/all_to_all | solution.py:73
  304.8 14.7 %copy-start.5 = (bf16[32,512]{1,0:T(8,128)(2,1)S(1)}, bf16[32,512]{1,0:T(8,128)(2,1)}, u32[]{:S(2)}) copy-start(bf16[32,512]{1,0:T(8,128)(2,1)} %copy-done.4) | copy-start | bytes 98308
  304.8 15.6 %copy-start.1 = (bf16[32,1024]{1,0:T(8,128)(2,1)S(1)}, bf16[32,1024]{1,0:T(8,128)(2,1)}, u32[]{:S(2)}) copy-start(bf16[32,1024]{1,0:T(8,128)(2,1)} %param.7) | copy-start | bytes 196612
Sparse Core Ops, SparseCore 0:
  76.5 88.3 all-reduce.2
  167.9 31.1 reduce-scatter.3
  206.4 30.6 all-gather.2
  238.8 30.6 all-gather.4
where the time goes:
time: 328 us; the launch traced here: 327 us
  waiting for transfers between devices  158 us (48%)
  matrix products  101 us (31%)
  local copies, waits for them, and re-layouts  22.4 us (7%)
  starting transfers between devices  19.4 us (6%)
  between operations  13.9 us (4%)
  other arithmetic  11.7 us (4%)
    psum x1, waiting for transfers between devices, local(): lax.psum(pre_gate.astype(jnp.bfloat16), 'tensor').astype(jnp.float32)  66 us
    unnamed x5, waiting for transfers between devices  28.6 us
    all_to_all x1, waiting for transfers between devices, local(): lax.all_to_all(token_send, 'expert', split_axis=0, concat_axis=1, tiled=T...  24.5 us
    all_gather x1, waiting for transfers between devices, local(): up_piece = lax.all_gather(up_grad, 'tensor', axis=2, tiled=True)  18.6 us
    dot_general x1, matrix products, local(): jnp.einsum('erf,edf->erd', up_piece, w_up, preferred_element_type=jnp.flo...  14 us
    unnamed x20, local copies, waits for them, and re-layouts  13.9 us
    dot_general x1, matrix products, local(): jnp.einsum('erf,erd->efd', hidden, grad_rows, preferred_element_type=jnp....  13.8 us
    dot_general x1, matrix products, local(): jnp.einsum('erf,edf->erd', gate_piece, w_gate, preferred_element_type=jnp...  13.8 us
  transfers between devices with their start and end apart: 8, of which 6 were waited for; matrix products, arithmetic and copies ran while one was open for 37% of the time, Pallas kernels for 0%

commit v1 on v0

--- a/solution.py
+++ b/solution.py
@@ -1,7 +1,15 @@
+import functools
 import jax
 import jax.numpy as jnp
 from jax import lax
 from jax.sharding import PartitionSpec as P
+
+
+def rows_mix(my_tile, row_axis):
+    return lax.all_gather(my_tile, row_axis).sum(axis=0)
+
+
+carry_halves = functools.partial(rows_mix, row_axis="tensor")
 
 
 def local(tokens, cotangent, expert_ids, route_weight, w_gate, w_up, w_down):
@@ -40,7 +48,7 @@
     pre_up = jnp.einsum("erd,edf->erf", token_rows, w_up, preferred_element_type=jnp.float32)
     slice_breadth = w_gate.shape[2] // lax.axis_size("tensor")
     gate_sum, up_sum = (
-        lax.psum(pre_gate.astype(jnp.bfloat16), "tensor").astype(jnp.float32),
+        carry_halves(pre_gate.astype(jnp.bfloat16)).astype(jnp.float32),
         lax.psum(pre_up.astype(jnp.bfloat16), "tensor").astype(jnp.float32),
     )
     sigmoid_all = jax.nn.sigmoid(gate_sum)

time: 328 us -> 360 us (1.098)
  waiting for transfers between devices: 158 us -> 188 us
    all_gather x0 -> x1, waiting for transfers between devices: none -> 69.9 us  [rows_mix(): return lax.all_gather(my_tile, row_axis).sum(axis=0)]
    psum x1, waiting for transfers between devices: 66 us -> 11.2 us  [local(): lax.psum(pre_up.astype(jnp.bfloat16), 'tensor').astype(jnp.float32)]
    all_to_all x1, waiting for transfers between devices: 0.01 us -> 12.6 us  [local(): lax.all_to_all(gradient_outgoing, 'expert', split_axis=0, concat_axis=1,...]
    reduce_sum x0 -> x1, other arithmetic: none -> 4.03 us  [rows_mix(): return lax.all_gather(my_tile, row_axis).sum(axis=0)]
    unnamed x5 -> x6, waiting for transfers between devices: 28.6 us -> 31.3 us
    unnamed x20 -> x12, local copies, waits for them, and re-layouts: 13.9 us -> 13.9 us
  transfers between devices with their start and end apart: 8 -> 9, of which waited for: 6 -> 8; matrix products, arithmetic and copies ran while one was open for 37% -> 34% of each run, Pallas kernels for 0% -> 0%
where the time goes in v1:
time: 360 us; the launch traced here: 359 us
  waiting for transfers between devices  188 us (52%)
  matrix products  102 us (28%)
  local copies, waits for them, and re-layouts  22.4 us (6%)
  starting transfers between devices  19.5 us (5%)
  between operations  13.9 us (4%)
  other arithmetic  12.3 us (3%)
    all_gather x1, waiting for transfers between devices, rows_mix(): return lax.all_gather(my_tile, row_axis).sum(axis=0)  69.9 us
    unnamed x6, waiting for transfers between devices  31.3 us
    all_to_all x1, waiting for transfers between devices, local(): lax.all_to_all(token_send, 'expert', split_axis=0, concat_axis=1, tiled=T...  24.5 us
    all_gather x1, waiting for transfers between devices, local(): up_piece = lax.all_gather(up_grad, 'tensor', axis=2, tiled=True)  18.6 us
    dot_general x1, matrix products, local(): jnp.einsum('erd,edf->erf', token_rows, w_gate, preferred_element_type=jnp...  14.1 us
    dot_general x1, matrix products, local(): jnp.einsum('erf,edf->erd', up_piece, w_up, preferred_element_type=jnp.flo...  14 us
    unnamed x12, local copies, waits for them, and re-layouts  13.9 us
    dot_general x1, matrix products, local(): jnp.einsum('erf,erd->efd', hidden, grad_rows, preferred_element_type=jnp....  13.8 us
  transfers between devices with their start and end apart: 9, of which 8 were waited for; matrix products, arithmetic and copies ran while one was open for 34% of the time, Pallas kernels for 0%

profile of v1, /device:TPU:0, one launch (start us, length us, event | category | flops | bytes accessed | tf_op | source)
XLA Modules:
  0.0 358.8 jit_solution(7566077223409970173)
XLA Ops:
  7.2 0.8 copy.45
  8.0 0.1 eq.43
  8.1 0.1 eq.39
  8.2 0.8 copy.49
  8.9 0.6 reduce-window.6
  9.6 0.2 slice_reduce_fusion
  9.8 0.1 fusion.17
  9.9 0.1 reduce_sum.42
  10.0 0.4 convert_reduce_fusion
  10.4 1.4 fusion
  11.8 6.4 %all-to-all-start = ((bf16[64,8,1024]{2,1,0:T(8,128)(2,1)}), bf16[64,8,1024]{2,1,0:T(8,128)(2,1)S(1)}, u32[]{:S(2)}, u32[]{:S(2)}) async-start(bf16[64,8,1024]{2,1,0:T(8,128)(2,1)} %fusion), calls=%async_computation | async-start | bytes 2097152 | tf_op jit(solution)/shard_map/all_to_all | solution.py:44
  18.2 2.0 fusion.1
  20.2 24.5 %all-to-all-done = bf16[64,8,1024]{2,1,0:T(8,128)(2,1)S(1)} async-done(((bf16[64,8,1024]{2,1,0:T(8,128)(2,1)}), bf16[64,8,1024]{2,1,0:T(8,128)(2,1)S(1)}, u32[]{:S(2)}, u32[]{:S(2)}) %all-to-all-start) | async-done | bytes 1048608 | tf_op jit(solution)/shard_map/all_to_all | solution.py:44
  44.8 3.6 all-to-all-start.2
  48.4 13.8 %convolution_convert_fusion.2 = bf16[8,64,1536]{2,1,0:T(8,128)(2,1)} fusion(bf16[8,1024,1536]{2,1,0:T(8,128)(2,1)} %param.12, bf16[8,8,8,1024]{3,2,1,0:T(8,128)(2,1)S(1)} %bitcast.69), kind=kOutput, calls=%fused_computation.4 | convolution fusion | flops 1611399168 | bytes 27787264 | tf_op jit(solution)/shard_map/erd,edf->erf/dot_general | solution.py:48
  62.2 12.6 %all-to-all-done.2 = bf16[64,8,1024]{2,1,0:T(8,128)(2,1)S(1)} async-done(((bf16[64,8,1024]{2,1,0:T(8,128)(2,1)}), bf16[64,8,1024]{2,1,0:T(8,128)(2,1)S(1)}, u32[]{:S(2)}, u32[]{:S(2)}) %all-to-all-start.2) | async-done | bytes 1048608 | tf_op jit(solution)/shard_map/all_to_all | solution.py:45
  74.8 13.8 %convolution_convert_fusion.1 = bf16[8,64,1536]{2,1,0:T(8,128)(2,1)} fusion(bf16[8,1536,1024]{2,1,0:T(8,128)(2,1)} %param.13, bf16[8,8,8,1024]{3,2,1,0:T(8,128)(2,1)S(1)} %bitcast.66), kind=kOutput, calls=%fused_computation.3 | convolution fusion | flops 1611399168 | bytes 27787264 | tf_op jit(solution)/shard_map/erd,efd->erf/dot_general | solution.py:64
  88.6 4.9 %copy.60 = bf16[8,64,1536]{1,0,2:T(8,128)(2,1)} copy(bf16[8,64,1536]{2,1,0:T(8,128)(2,1)} %convolution_convert_fusion.1) | data formatting | bytes 3145728
  93.4 5.4 %reshape.62 = bf16[1536,512]{1,0:T(8,128)(2,1)} reshape(bf16[1536,8,64]{2,1,0:T(8,128)(2,1)} %bitcast.68) | data formatting | bytes 3145728
  98.9 0.0 all-gather.9.cloned.1.call-start
  98.9 14.1 %convolution_convert_fusion.3 = bf16[8,64,1536]{2,1,0:T(8,128)(2,1)} fusion(bf16[8,1024,1536]{2,1,0:T(8,128)(2,1)} %param.11, bf16[8,8,8,1024]{3,2,1,0:T(8,128)(2,1)S(1)} %bitcast.70), kind=kOutput, calls=%fused_computation.5 | convolution fusion | flops 1611399168 | bytes 27787264 | tf_op jit(solution)/shard_map/erd,edf->erf/dot_general | solution.py:47
  113.0 0.2 all-gather.5.cloned.1.call-start
  113.2 11.2 %all-reduce.2.cloned.1.call-done = bf16[8,64,1536]{2,1,0:T(8,128)(2,1)} async-done(((bf16[8,64,1536]{2,1,0:T(8,128)(2,1)}), bf16[8,64,1536]{2,1,0:T(8,128)(2,1)}) %all-reduce.2.cloned.1.call-update) | async-done | bytes 1572880 | tf_op jit(solution)/shard_map/psum | solution.py:52
  124.4 3.5 convert_element_type.74
  127.9 30.7 %reduce-scatter.4.cloned.1.call-done = bf16[384,512]{1,0:T(8,128)(2,1)} async-done(((bf16[1536,512]{1,0:T(8,128)(2,1)}), bf16[384,512]{1,0:T(8,128)(2,1)}) %reduce-scatter.4.cloned.1.call-update) | async-done | bytes 393232
  158.6 1.5 reshape.63
  160.1 0.5 copy.61
  160.6 69.9 %all-gather.9.cloned.1.call-done = bf16[32,64,1536]{2,1,0:T(8,128)(2,1)} async-done(((bf16[8,64,1536]{2,1,0:T(8,128)(2,1)}), bf16[32,64,1536]{2,1,0:T(8,128)(2,1)}) %all-gather.9.cloned.1.call-update) | async-done | bytes 6291472 | tf_op jit(solution)/shard_map/all_gather | solution.py:9
  230.5 4.0 %reduce_sum.45 = bf16[8,64,1536]{2,1,0:T(8,128)(2,1)S(1)} reduce(bf16[4,8,64,1536]{3,2,1,0:T(8,128)(2,1)} %bitcast.71, bf16[]{:T(256)} %constant.7.clone.1), dimensions={0}, to_apply=%region_5.6 | reduce | flops 2359296 | bytes 7864322 | tf_op jit(solution)/shard_map/reduce_sum | solution.py:9
  234.5 0.8 add_divide_fusion
  235.3 0.4 convert_element_type.72
  235.7 2.4 fusion.14
  238.2 0.5 all-gather.7.cloned.1.call-update
  238.7 13.5 %convolution_convert_fusion.4 = bf16[8,64,1024]{2,1,0:T(8,128)(2,1)S(1)} fusion(bf16[8,1536,1024]{2,1,0:T(8,128)(2,1)} %param.13, bf16[8,64,1536]{2,1,0:T(8,128)(2,1)S(1)} %reduce_sum.45, bf16[8,64,1536]{2,1,0:T(8,128)(2,1)} %all-reduce.2.cloned.1.call-done), kind=kOutput, calls=%fused_computation.7 | convolution fusion | flops 1617428480 | bytes 29360128 | tf_op jit(solution)/shard_map/erf,efd->erd/dot_general | solution.py:56
  252.3 1.5 copy.51
  253.8 4.6 %all-to-all-start.1 = ((bf16[8,64,1024]{2,0,1:T(8,128)(2,1)}), bf16[8,64,1024]{2,0,1:T(8,128)(2,1)}, u32[]{:S(2)}, u32[]{:S(2)}) async-start(bf16[8,64,1024]{2,0,1:T(8,128)(2,1)} %copy.51), calls=%async_computation.1 | async-start | bytes 2097152 | tf_op jit(solution)/shard_map/all_to_all | solution.py:80
  258.4 10.6 %all-gather.5.cloned.1.call-done = bf16[8,64,1536]{2,1,0:T(8,128)(2,1)} async-done(((bf16[8,64,384]{2,1,0:T(8,128)(2,1)}), bf16[8,64,1536]{2,1,0:T(8,128)(2,1)}) %all-gather.5.cloned.1.call-update) | async-done | bytes 1572880 | tf_op jit(solution)/shard_map/all_gather | solution.py:72
  269.0 13.8 %fusion.21 = f32[8,64,1024]{2,1,0:T(8,128)} fusion(bf16[8,64,1536]{2,1,0:T(8,128)(2,1)} %all-gather.5.cloned.1.call-done, bf16[8,1024,1536]{2,1,0:T(8,128)(2,1)} %param.11), kind=kOutput, calls=%fused_computation.44 | convolution fusion | flops 1610612736 | bytes 28835840 | tf_op jit(solution)/shard_map/erf,edf->erd/dot_general | solution.py:74
  282.8 18.6 %all-gather.7.cloned.1.call-done = bf16[8,64,1536]{2,1,0:T(8,128)(2,1)} async-done(((bf16[8,64,384]{2,1,0:T(8,128)(2,1)}), bf16[8,64,1536]{2,1,0:T(8,128)(2,1)}) %all-gather.7.cloned.1.call-update) | async-done | bytes 1572880 | tf_op jit(solution)/shard_map/all_gather | solution.py:73
  301.4 14.0 %add_convert_fusion = bf16[8,64,1024]{2,1,0:T(8,128)(2,1)} fusion(f32[8,64,1024]{2,1,0:T(8,128)} %fusion.21, bf16[8,64,1536]{2,1,0:T(8,128)(2,1)} %all-gather.7.cloned.1.call-done, bf16[8,1024,1536]{2,1,0:T(8,128)(2,1)} %param.12), kind=kOutput, calls=%fused_computation.6 | convolution fusion | flops 1611661312 | bytes 29884416 | tf_op jit(solution)/shard_map/erf,edf->erd/dot_general | solution.py:75
  315.4 2.8 copy.55
  318.2 4.6 %all-to-all-start.3 = ((bf16[8,64,1024]{2,0,1:T(8,128)(2,1)}), bf16[8,64,1024]{2,0,1:T(8,128)(2,1)}, u32[]{:S(2)}, u32[]{:S(2)}) async-start(bf16[8,64,1024]{2,0,1:T(8,128)(2,1)} %copy.55), calls=%async_computation.3 | async-start | bytes 2097152 | tf_op jit(solution)/shard_map/all_to_all | solution.py:81
  322.8 13.8 %convolution_convert_fusion = bf16[8,1536,1024]{2,1,0:T(8,128)(2,1)} fusion(bf16[8,8,8,1024]{3,2,1,0:T(8,128)(2,1)S(1)} %bitcast.67, bf16[8,64,1536]{2,1,0:T(8,128)(2,1)S(1)} %reduce_sum.45, bf16[8,64,1536]{2,1,0:T(8,128)(2,1)} %all-reduce.2.cloned.1.call-done), kind=kOutput, calls=%fused_computation | convolution fusion | flops 1629487104 | bytes 29360128 | tf_op jit(solution)/shard_map/erf,erd->efd/dot_general | solution.py:59
  336.6 1.9 copy.53
  338.5 1.2 convolution_convert_fusion.8
  339.7 9.8 %all-to-all-done.3 = bf16[8,64,1024]{2,0,1:T(8,128)(2,1)} async-done(((bf16[8,64,1024]{2,0,1:T(8,128)(2,1)}), bf16[8,64,1024]{2,0,1:T(8,128)(2,1)}, u32[]{:S(2)}, u32[]{:S(2)}) %all-to-all-start.3) | async-done | bytes 1048608 | tf_op jit(solution)/shard_map/all_to_all | solution.py:81
  349.5 1.8 copy.57
  351.3 0.9 convolution_convert_fusion.7
  (18 shorter events, 0.3 us)
Async XLA Ops:
  7.2 3.2 copy-start
  7.2 11.0 %copy-start.2 = (bf16[32,1024]{1,0:T(8,128)(2,1)S(1)}, bf16[32,1024]{1,0:T(8,128)(2,1)}, u32[]{:S(2)}) copy-start(bf16[32,1024]{1,0:T(8,128)(2,1)} %param.8) | copy-start | bytes 196612
  11.8 32.9 %all-to-all-start = ((bf16[64,8,1024]{2,1,0:T(8,128)(2,1)}), bf16[64,8,1024]{2,1,0:T(8,128)(2,1)S(1)}, u32[]{:S(2)}, u32[]{:S(2)}) async-start(bf16[64,8,1024]{2,1,0:T(8,128)(2,1)} %fusion), calls=%async_computation | async-start | bytes 2097152 | tf_op jit(solution)/shard_map/all_to_all | solution.py:44
  44.8 30.1 %all-to-all-start.2 = ((bf16[64,8,1024]{2,1,0:T(8,128)(2,1)}), bf16[64,8,1024]{2,1,0:T(8,128)(2,1)S(1)}, u32[]{:S(2)}, u32[]{:S(2)}) async-start(bf16[64,8,1024]{2,1,0:T(8,128)(2,1)} %fusion.1), calls=%async_computation.2 | async-start | bytes 2097152 | tf_op jit(solution)/shard_map/all_to_all | solution.py:45
  48.3 76.1 %all-reduce.2.cloned.1.call-start = ((), (), s32[]{:S(2)}) async-start(), calls=%async_computation.5 | async-start | bytes 3145728 | tf_op jit(solution)/shard_map/psum | solution.py:52
  62.1 96.4 %reduce-scatter.4.cloned.1.call-start = ((), (), s32[]{:S(2)}) async-start(), calls=%async_computation.9 | async-start | bytes 1966080
  98.9 131.6 %all-gather.9.cloned.1.call-start = ((), (), s32[]{:S(2)}) async-start(), calls=%async_computation.8 | async-start | bytes 7864320 | tf_op jit(solution)/shard_map/all_gather | solution.py:9
  113.0 156.0 %all-gather.5.cloned.1.call-start = ((), (), s32[]{:S(2)}) async-start(), calls=%async_computation.6 | async-start | bytes 1966080 | tf_op jit(solution)/shard_map/all_gather | solution.py:72
  238.2 63.3 %all-gather.7.cloned.1.call-start = ((), (), s32[]{:S(2)}) async-start(), calls=%async_computation.7 | async-start | bytes 1966080 | tf_op jit(solution)/shard_map/all_gather | solution.py:73
  253.8 64.4 %all-to-all-start.1 = ((bf16[8,64,1024]{2,0,1:T(8,128)(2,1)}), bf16[8,64,1024]{2,0,1:T(8,128)(2,1)}, u32[]{:S(2)}, u32[]{:S(2)}) async-start(bf16[8,64,1024]{2,0,1:T(8,128)(2,1)} %copy.51), calls=%async_computation.1 | async-start | bytes 2097152 | tf_op jit(solution)/shard_map/all_to_all | solution.py:80
  318.2 31.3 %all-to-all-start.3 = ((bf16[8,64,1024]{2,0,1:T(8,128)(2,1)}), bf16[8,64,1024]{2,0,1:T(8,128)(2,1)}, u32[]{:S(2)}, u32[]{:S(2)}) async-start(bf16[8,64,1024]{2,0,1:T(8,128)(2,1)} %copy.55), calls=%async_computation.3 | async-start | bytes 2097152 | tf_op jit(solution)/shard_map/all_to_all | solution.py:81
  336.6 15.6 %copy-start.1 = (bf16[32,1024]{1,0:T(8,128)(2,1)S(1)}, bf16[32,1024]{1,0:T(8,128)(2,1)}, u32[]{:S(2)}) copy-start(bf16[32,1024]{1,0:T(8,128)(2,1)} %param.7) | copy-start | bytes 196612
Sparse Core Ops, SparseCore 0:
  62.3 62.0 all-reduce.1
  127.4 31.1 reduce-scatter.3
  160.4 70.0 all-gather.8
  238.3 30.6 all-gather.4
  270.7 30.6 all-gather.6
